TPU v7x, 128 devices: a whole 4x4x4 slice. The times are simulated.
128 devices in a mesh: rep: 4 (over x_hi, core), shard: 32 (over y, x_lo, z).
Axes of the slice: x: 4 (x_hi: 2, x_lo: 2; x = x_hi * 2 + x_lo), y: 4, z: 4, core: 2. Of those that a mesh axis runs over, the one named last changes fastest.
Arguments:
- inputs: bfloat16 [128, 128, 1024], P(('rep', 'shard')), may hold values from -6 to 6
- lengths: int32 [128], P(('rep', 'shard')), may hold values from 32 to 128, as said below
- cotangent: bfloat16 [128, 128, 1024], P(('rep', 'shard')), may hold values from -6 to 6
- w_qkv: bfloat16 [1, 1024, 3072], P(None, 'shard'), may hold values from -0.1875 to 0.1875
- b_qv: bfloat16 [1, 2, 1024], P(None, None, 'shard'), may hold values from -4 to 4
- w_att: bfloat16 [1, 1024, 1024], P(None, 'shard'), may hold values from -1 to 1
- b_att: bfloat16 [1, 1024], P(None, 'shard'), may hold values from -4 to 4
- norm1_gain: bfloat16 [1, 1024], P(None, 'shard'), may hold values from 0.5 to 1.5
- norm1_bias: bfloat16 [1, 1024], P(None, 'shard'), may hold values from -4 to 4
- w_in: bfloat16 [1, 1024, 4096], P(None, 'shard'), may hold values from -0.1875 to 0.1875
- b_in: bfloat16 [1, 4096], P(None, 'shard'), may hold values from -4 to 4
- w_out: bfloat16 [1, 4096, 1024], P(None, 'shard'), may hold values from -0.09375 to 0.09375
- b_out: bfloat16 [1, 1024], P(None, 'shard'), may hold values from -4 to 4
- norm2_gain: bfloat16 [1, 1024], P(None, 'shard'), may hold values from 0.5 to 1.5
- norm2_bias: bfloat16 [1, 1024], P(None, 'shard'), may hold values from -4 to 4
Outputs:
- outputs: bfloat16 [128, 128, 1024], P(('rep', 'shard'))
- grad_inputs: float32 [128, 128, 1024], P(('rep', 'shard'))
- grad_w_qkv: float32 [1, 1024, 3072], P(None, 'shard')
- grad_b_qv: float32 [1, 2, 1024], P(None, None, 'shard')
- grad_w_att: float32 [1, 1024, 1024], P(None, 'shard')
- grad_b_att: float32 [1, 1024], P(None, 'shard')
- grad_norm1_gain: float32 [1, 1024], P(None, 'shard')
- grad_norm1_bias: float32 [1, 1024], P(None, 'shard')
- grad_w_in: float32 [1, 1024, 4096], P(None, 'shard')
- grad_b_in: float32 [1, 4096], P(None, 'shard')
- grad_w_out: float32 [1, 4096, 1024], P(None, 'shard')
- grad_b_out: float32 [1, 1024], P(None, 'shard')
- grad_norm2_gain: float32 [1, 1024], P(None, 'shard')
- grad_norm2_bias: float32 [1, 1024], P(None, 'shard')
Inputs may be any that keep to these rules, and one draw needn't show every extreme that they name: `lengths`: some sequence has all 128 positions valid.
All inputs are finite; a program needn't handle non-finite values.
Results may differ from a plain program's by a relative error of at most 0.013.
Values may be sent and summed in bfloat16 or wider, within the bound.
No kernel may reach another device: no remote copies, remote signals or barrier semaphores. Data moves between devices by JAX's collectives and lax.ppermute only.
A program may use at most 192 MiB of HBM per device.

v0:
```python
import math
import jax
import jax.numpy as jnp
from jax import lax
from jax.sharding import PartitionSpec as P

HEAD_DIM = 64
LAYERS = 1
EPS = 1e-12
ROOT_HALF = 0.7071067811865476
INV_ROOT_TWO_PI = 0.3989422804014327


def sent_together(arrays, axis, dim, along):
    columns = [a.reshape(*a.shape[:along], -1) for a in arrays]
    both = jnp.concatenate(columns, axis=along)
    filled, at, done = (lax.all_gather(both, axis, axis=dim, tiled=True), 0, [])
    for a, column in zip(arrays, columns):
        share = filled[..., at : at + column.shape[along]]
        done.append(share.reshape(*share.shape[:along], *a.shape[along:]))
        at += column.shape[along]
    return tuple(done)


def in_one_piece(arrays, axis, dim, along):
    columns = [a.reshape(*a.shape[:along], -1) for a in arrays]
    both = jnp.concatenate(columns, axis=along)
    filled, at, done = (lax.psum_scatter(both, axis, scatter_dimension=dim, tiled=True), 0, [])
    for a, column in zip(arrays, columns):
        share = filled[..., at : at + column.shape[along]]
        done.append(share.reshape(*share.shape[:along], *a.shape[along:]))
        at += column.shape[along]
    return tuple(done)


def together(arrays, axis):
    line, at, done = (jnp.concatenate([a.reshape(-1) for a in arrays]), 0, [])
    so_far = lax.psum(line, axis)
    for a in arrays:
        done.append(so_far[at : at + a.size].reshape(a.shape))
        at += a.size
    return tuple(done)


def batched(form, left, right):
    return jnp.einsum(form, left, right, preferred_element_type=jnp.float32)


def layer_norm(residual, gain, shift):
    row_mean = jnp.mean(residual, axis=-1, keepdims=True)
    centered = residual - row_mean
    variance = jnp.mean(centered * centered, axis=-1, keepdims=True)
    inv_std = lax.rsqrt(variance + EPS)
    normed = centered * inv_std
    return (normed * gain.astype(jnp.float32) + shift.astype(jnp.float32), normed, inv_std)


def norm_backward(upstream, normed, inv_std, gain):
    grad_gain = jnp.sum(upstream * normed, axis=0)
    grad_shift = jnp.sum(upstream, axis=0)
    scaled = upstream * gain.astype(jnp.float32)
    grad_res = inv_std * (
        scaled
        - jnp.mean(scaled, axis=-1, keepdims=True)
        - normed * jnp.mean(scaled * normed, axis=-1, keepdims=True)
    )
    return (grad_res, grad_gain, grad_shift)


def attention_scores(query_bf, key_bf, key_valid):
    scores = batched("bqhe,bkhe->bhqk", query_bf, key_bf) * (1.0 / math.sqrt(HEAD_DIM))
    return jnp.where(key_valid[:, None, None, :], scores, -1e30)


def layer_forward(hidden, hidden_bf, params, key_valid, batch_size):
    (
        w_qkv,
        b_qv,
        w_att,
        b_att,
        gain_one,
        shift_one,
        w_in,
        b_in,
        w_out,
        b_out,
        gain_two,
        shift_two,
    ) = params
    model_width = hidden.shape[1]
    seq_count = hidden.shape[0] // batch_size
    shape_heads = (batch_size, seq_count, model_width // HEAD_DIM, HEAD_DIM)
    packed = jnp.dot(hidden_bf, w_qkv, preferred_element_type=jnp.float32)
    bias_qv = b_qv.astype(jnp.float32)
    query_bf = (packed[:, :model_width] + bias_qv[0]).astype(jnp.bfloat16).reshape(shape_heads)
    key_bf = packed[:, model_width : 2 * model_width].astype(jnp.bfloat16).reshape(shape_heads)
    value_bf = (packed[:, 2 * model_width :] + bias_qv[1]).astype(jnp.bfloat16).reshape(shape_heads)
    scores = attention_scores(query_bf, key_bf, key_valid)
    row_max = jnp.max(scores, axis=-1, keepdims=True)
    row_lse = row_max + jnp.log(jnp.sum(jnp.exp(scores - row_max), axis=-1, keepdims=True))
    probs_bf = jnp.exp(scores - row_lse).astype(jnp.bfloat16)
    context_bf = (
        batched("bhqk,bkhe->bqhe", probs_bf, value_bf).astype(jnp.bfloat16).reshape(-1, model_width)
    )
    first = (
        hidden
        + jnp.dot(context_bf, w_att, preferred_element_type=jnp.float32)
        + b_att.astype(jnp.float32)
    )
    middle, normed_one, inv_one = layer_norm(first, gain_one, shift_one)
    middle_bf = middle.astype(jnp.bfloat16)
    pre_act = jnp.dot(middle_bf, w_in, preferred_element_type=jnp.float32) + b_in.astype(
        jnp.float32
    )
    act_bf = (pre_act * 0.5 * (1.0 + jax.scipy.special.erf(pre_act * ROOT_HALF))).astype(
        jnp.bfloat16
    )
    second = (
        middle
        + jnp.dot(act_bf, w_out, preferred_element_type=jnp.float32)
        + b_out.astype(jnp.float32)
    )
    result, normed_two, inv_two = layer_norm(second, gain_two, shift_two)
    stored = (
        hidden_bf,
        query_bf,
        key_bf,
        value_bf,
        row_lse,
        context_bf,
        normed_one,
        inv_one,
        middle_bf,
        pre_act,
        act_bf,
        normed_two,
        inv_two,
    )
    return (result, stored)


def layer_backward(upstream, stored, params, key_valid):
    (
        w_qkv,
        b_qv,
        w_att,
        b_att,
        gain_one,
        shift_one,
        w_in,
        b_in,
        w_out,
        b_out,
        gain_two,
        shift_two,
    ) = params
    (
        hidden_bf,
        query_bf,
        key_bf,
        value_bf,
        row_lse,
        context_bf,
        normed_one,
        inv_one,
        middle_bf,
        pre_act,
        act_bf,
        normed_two,
        inv_two,
    ) = stored
    model_width = upstream.shape[1]
    shape_heads = query_bf.shape
    grad_second, grad_gain_two, grad_shift_two = norm_backward(
        upstream, normed_two, inv_two, gain_two
    )
    grad_b_out = jnp.sum(grad_second, axis=0)
    second_bf = grad_second.astype(jnp.bfloat16)
    grad_w_out = jnp.dot(act_bf.T, second_bf, preferred_element_type=jnp.float32)
    back_act = jnp.dot(second_bf, w_out.T, preferred_element_type=jnp.float32)
    cumulative = 0.5 * (1.0 + jax.scipy.special.erf(pre_act * ROOT_HALF))
    density = jnp.exp(-0.5 * pre_act * pre_act) * INV_ROOT_TWO_PI
    grad_pre = back_act * (cumulative + pre_act * density)
    pre_bf = grad_pre.astype(jnp.bfloat16)
    grad_w_in = jnp.dot(middle_bf.T, pre_bf, preferred_element_type=jnp.float32)
    grad_b_in = jnp.sum(grad_pre, axis=0)
    grad_middle = grad_second + jnp.dot(pre_bf, w_in.T, preferred_element_type=jnp.float32)
    grad_first, grad_gain_one, grad_shift_one = norm_backward(
        grad_middle, normed_one, inv_one, gain_one
    )
    grad_b_att = jnp.sum(grad_first, axis=0)
    first_bf = grad_first.astype(jnp.bfloat16)
    grad_w_att = jnp.dot(context_bf.T, first_bf, preferred_element_type=jnp.float32)
    grad_context = (
        jnp.dot(first_bf, w_att.T, preferred_element_type=jnp.float32)
        .astype(jnp.bfloat16)
        .reshape(shape_heads)
    )
    scores = attention_scores(query_bf, key_bf, key_valid)
    probs = jnp.exp(scores - row_lse)
    grad_value = batched("bhqk,bqhe->bkhe", probs.astype(jnp.bfloat16), grad_context).reshape(
        -1, model_width
    )
    grad_probs = batched("bqhe,bkhe->bhqk", grad_context, value_bf)
    inner = jnp.sum(probs * grad_probs, axis=-1, keepdims=True)
    grad_scores = (probs * (grad_probs - inner) * (1.0 / math.sqrt(HEAD_DIM))).astype(jnp.bfloat16)
    grad_query = batched("bhqk,bkhe->bqhe", grad_scores, key_bf).reshape(-1, model_width)
    grad_key = batched("bhqk,bqhe->bkhe", grad_scores, query_bf).reshape(-1, model_width)
    grad_b_qv = jnp.stack([jnp.sum(grad_query, axis=0), jnp.sum(grad_value, axis=0)])
    packed_bf = jnp.concatenate([grad_query, grad_key, grad_value], axis=1).astype(jnp.bfloat16)
    grad_w_qkv = jnp.dot(hidden_bf.T, packed_bf, preferred_element_type=jnp.float32)
    grad_hidden = grad_first + jnp.dot(packed_bf, w_qkv.T, preferred_element_type=jnp.float32)
    terms = (
        grad_w_qkv,
        grad_b_qv,
        grad_w_att,
        grad_b_att,
        grad_gain_one,
        grad_shift_one,
        grad_w_in,
        grad_b_in,
        grad_w_out,
        grad_b_out,
        grad_gain_two,
        grad_shift_two,
    )
    return (grad_hidden, terms)


def body(
    inputs,
    lengths,
    cotangent,
    w_qkv,
    b_qv,
    w_att,
    b_att,
    norm1_gain,
    norm1_bias,
    w_in,
    b_in,
    w_out,
    b_out,
    norm2_gain,
    norm2_bias,
):
    batch_size, seq_count, model_width = inputs.shape
    key_valid = lax.broadcasted_iota(jnp.int32, (batch_size, seq_count), 1) < lengths[:, None]
    hidden = inputs.astype(jnp.float32).reshape(-1, model_width)
    hidden_bf = inputs.reshape(-1, model_width)
    kept_params = []
    layer_index = 0
    params = (
        lax.all_gather(w_qkv[layer_index], "shard", axis=0, tiled=True),
        lax.all_gather(b_qv[layer_index], "shard", axis=1, tiled=True),
        *sent_together(
            (
                w_att[layer_index],
                b_att[layer_index],
                norm1_gain[layer_index],
                norm1_bias[layer_index],
                w_in[layer_index],
            ),
            "shard",
            0,
            1,
        ),
        *sent_together((b_in[layer_index], w_out[layer_index]), "shard", 0, 1),
        lax.all_gather(b_out[layer_index], "shard", axis=0, tiled=True),
        lax.all_gather(norm2_gain[layer_index], "shard", axis=0, tiled=True),
        lax.all_gather(norm2_bias[layer_index], "shard", axis=0, tiled=True),
    )
    hidden, stored = layer_forward(hidden, hidden_bf, params, key_valid, batch_size)
    hidden_bf = hidden.astype(jnp.bfloat16)
    kept_params.append(params)
    stored_list = [stored]
    outputs = hidden_bf.reshape(inputs.shape)
    upstream = cotangent.astype(jnp.float32).reshape(-1, model_width)
    owned = [None] * LAYERS
    for layer_index in reversed(range(LAYERS)):
        params = (
            lax.all_gather(w_qkv[layer_index], "shard", axis=0, tiled=True),
            lax.all_gather(b_qv[layer_index], "shard", axis=1, tiled=True),
            *sent_together(
                (
                    w_att[layer_index],
                    b_att[layer_index],
                    norm1_gain[layer_index],
                    norm1_bias[layer_index],
                    w_in[layer_index],
                ),
                "shard",
                0,
                1,
            ),
            *sent_together((b_in[layer_index], w_out[layer_index]), "shard", 0, 1),
            lax.all_gather(b_out[layer_index], "shard", axis=0, tiled=True),
            lax.all_gather(norm2_gain[layer_index], "shard", axis=0, tiled=True),
            lax.all_gather(norm2_bias[layer_index], "shard", axis=0, tiled=True),
        )
        upstream, terms = layer_backward(upstream, stored_list[layer_index], params, key_valid)
        shares = (
            lax.psum_scatter(terms[0], "shard", scatter_dimension=0, tiled=True),
            lax.psum_scatter(terms[1], "shard", scatter_dimension=1, tiled=True),
            *in_one_piece((terms[2], terms[3], terms[4], terms[5], terms[6]), "shard", 0, 1),
            *in_one_piece((terms[7], terms[8]), "shard", 0, 1),
            lax.psum_scatter(terms[9], "shard", scatter_dimension=0, tiled=True),
            lax.psum_scatter(terms[10], "shard", scatter_dimension=0, tiled=True),
            lax.psum_scatter(terms[11], "shard", scatter_dimension=0, tiled=True),
        )
        shares = together(
            (
                shares[0],
                shares[1],
                shares[2],
                shares[3],
                shares[4],
                shares[5],
                shares[6],
                shares[7],
                shares[8],
                shares[9],
                shares[10],
                shares[11],
            ),
            "rep",
        )
        owned[layer_index] = shares
    final = [jnp.stack([owned[0][member]]) for member in range(12)]
    grad_inputs = upstream.reshape(inputs.shape)
    return (
        outputs,
        grad_inputs,
        final[0],
        final[1],
        final[2],
        final[3],
        final[4],
        final[5],
        final[6],
        final[7],
        final[8],
        final[9],
        final[10],
        final[11],
    )


def solution(mesh):
    return jax.shard_map(
        body,
        mesh=mesh,
        in_specs=(
            P(("rep", "shard"), None, None),
            P(("rep", "shard")),
            P(("rep", "shard"), None, None),
            P(None, "shard", None),
            P(None, None, "shard"),
            P(None, "shard", None),
            P(None, "shard"),
            P(None, "shard"),
            P(None, "shard"),
            P(None, "shard", None),
            P(None, "shard"),
            P(None, "shard", None),
            P(None, "shard"),
            P(None, "shard"),
            P(None, "shard"),
        ),
        out_specs=(
            P(("rep", "shard"), None, None),
            P(("rep", "shard"), None, None),
            P(None, "shard", None),
            P(None, None, "shard"),
            P(None, "shard", None),
            P(None, "shard"),
            P(None, "shard"),
            P(None, "shard"),
            P(None, "shard", None),
            P(None, "shard"),
            P(None, "shard", None),
            P(None, "shard"),
            P(None, "shard"),
            P(None, "shard"),
        ),
        check_vma=False,
    )
```

profile of v0, /device:TPU:1, one launch (start us, length us, event | category | flops | bytes accessed | tf_op | source)
XLA Modules:
  0.0 1430.6 jit_solution(17285094910690135515)
XLA Ops:
  7.3 0.7 all-gather.13.cloned.1.call-update
  8.0 0.8 copy.91
  8.8 1.8 pad_maximum_fusion.4
  10.7 0.8 copy.88
  11.4 0.8 copy.89
  12.2 0.8 copy.90
  12.9 2.0 concatenate.21
  15.7 0.6 fusion.108
  17.6 74.4 %all-reduce.7 = (bf16[1024]{0:T(1024)(128)(2,1)S(1)}, bf16[1024]{0:T(1024)(128)(2,1)S(1)}, bf16[1024]{0:T(1024)(128)(2,1)S(1)}) all-reduce(bf16[1024]{0:T(1024)(128)(2,1)S(1)} %dynamic-update-slice, bf16[1024]{0:T(1024)(128)(2,1)S(1)} %dynamic-update-slice.2, ...), channel_id=4, replica_groups=mesh['rep'=4,'shard'=32] {'shard'}, use_global_device_ids=true, to_apply=%add | all-reduce | flops 3072 | bytes 12288
  92.2 68.2 %all-gather.1 = bf16[1,2,1024]{1,0,2:T(2,128)(2,1)S(1)} all-gather(bf16[1,2,32]{1,0,2:T(2,128)(2,1)S(1)} %copy.83), channel_id=3, replica_groups=mesh['rep'=4,'shard'=32] {'shard'}, dimensions={2}, use_global_device_ids=true | all-gather | bytes 4224 | tf_op jit(solution)/shard_map/all_gather | solution.py:255
  160.4 0.5 convert_element_type.136
  161.0 7.2 slice_reduce_fusion
  168.2 3.8 fusion.11
  172.7 0.4 fusion.109
  173.3 0.3 convolution_convert_fusion.1
  173.6 156.3 %all-gather.11.cloned.1.call-done = bf16[4096,1025]{1,0:T(8,128)(2,1)} async-done(((bf16[128,1025]{1,0:T(8,128)(2,1)}), bf16[4096,1025]{1,0:T(8,128)(2,1)}) %all-gather.11.cloned.1.call-update) | async-done | bytes 8396816 | tf_op jit(solution)/shard_map/all_gather | solution.py:17
  329.9 1.6 convert_reduce_fusion
  331.5 174.2 %all-gather.9.cloned.1.call-done = bf16[1024,5123]{1,0:T(8,128)(2,1)} async-done(((bf16[32,5123]{1,0:T(8,128)(2,1)}), bf16[1024,5123]{1,0:T(8,128)(2,1)}) %all-gather.9.cloned.1.call-update) | async-done | bytes 10491920 | tf_op jit(solution)/shard_map/all_gather | solution.py:17
  505.7 1.6 convert_reduce_fusion.3
  507.3 2.1 fusion.110
  509.7 6.9 fusion.13
  516.7 3.2 fusion.111
  520.2 0.3 fusion.70
  520.5 1.0 fusion.102
  521.4 4.3 fusion.114
  525.8 3.7 multiply_reduce_fusion.1
  529.8 0.8 fusion.53
  530.8 0.6 fusion.107
  531.3 1.3 fusion.115
  532.7 2.1 convolution_convert_fusion
  534.8 2.3 fusion.106
  537.2 1.0 copy.109
  538.5 6.4 convolution_bitcast_fusion
  544.9 12.6 copy.107
  557.6 1.0 copy-done.6
  558.5 4.0 fusion.91
  562.5 6.4 pad_maximum_fusion
  569.9 2.7 fusion.88
  572.5 8.3 fusion.73
  580.8 25.0 %concatenate.24 = f32[1024,5123]{1,0:T(8,128)} concatenate(f32[1024,1024]{1,0:T(8,128)} %fusion.88, f32[1024,1]{1,0:T(8,128)S(1)} %copy.98, f32[1024,1]{1,0:T(8,128)S(1)} %copy.99, f32[1024,1]{1,0:T(8,128)S(1)} %copy.100, f32[1024,4096]{1,0:T(8,128)} %fusion.73), dimensions={1} | concatenate | bytes 41967616 | tf_op jit(solution)/shard_map/concatenate | solution.py:27
  606.6 131.1 %all-reduce.6 = (f32[1024]{0:T(1024)S(1)}, f32[1024]{0:T(1024)S(1)}, f32[1024]{0:T(1024)S(1)}) all-reduce(f32[1024]{0:T(1024)S(1)} %get-tuple-element.35, f32[1024]{0:T(1024)S(1)} %get-tuple-element.19, f32[1024]{0:T(1024)S(1)} %convert_reduce_fusion.1), channel_id=11, replica_groups=mesh['rep'=4,'shard'=32] {'shard'}, use_global_device_ids=true, to_apply=%region_22.23.clone | all-reduce | flops 3072 | bytes 24576
  738.0 0.8 copy.110
  738.8 143.8 %reduce-scatter.13.cloned.1.call-done = f32[32,3072]{1,0:T(8,128)} async-done(((f32[1024,3072]{1,0:T(8,128)}), f32[32,3072]{1,0:T(8,128)}) %reduce-scatter.13.cloned.1.call-update) | async-done | bytes 393232 | tf_op jit(solution)/shard_map/reduce_scatter | solution.py:303
  882.6 1.1 copy.111
  883.7 205.5 %reduce-scatter.11.cloned.1.call-done = f32[128,1025]{0,1:T(8,128)} async-done(((f32[4096,1025]{0,1:T(8,128)}), f32[128,1025]{0,1:T(8,128)}) %reduce-scatter.11.cloned.1.call-update) | async-done | bytes 524816 | tf_op jit(solution)/shard_map/reduce_scatter | solution.py:28
  1089.2 1.1 slice.157
  1090.6 0.7 slice_bitcast_fusion.9
  1091.2 255.8 %reduce-scatter.9.cloned.1.call-done = f32[32,5123]{1,0:T(8,128)} async-done(((f32[1024,5123]{1,0:T(8,128)}), f32[32,5123]{1,0:T(8,128)}) %reduce-scatter.9.cloned.1.call-update) | async-done | bytes 655760 | tf_op jit(solution)/shard_map/reduce_scatter | solution.py:28
  1347.0 1.2 slice_bitcast_fusion
  1348.4 0.9 slice_bitcast_fusion.1
  1349.3 1.1 slice_reduce_fusion.2
  1350.4 16.6 %concatenate.26 = f32[393600]{0:T(1024)} concatenate(f32[98304]{0:T(1024)S(1)} %bitcast.137, f32[64]{0:T(128)S(1)} %reshape.292, f32[32768]{0:T(1024)S(1)} %bitcast.148, f32[32]{0:T(128)S(1)} %get-tuple-element.23, f32[32]{0:T(128)S(1)} %get-tuple-element.22, f32[32]{0:T(128)S(1)} %get-tuple-element.21, f32[131072]{0:T(1024)S(1)} %bitcast.136, f32[128]{0:T(128)S(1)} %slice_bitcast_fusion.9, ...), dimensions={0} | concatenate | bytes 3148800 | tf_op jit(solution)/shard_map/concatenate | solution.py:37
  1367.1 5.8 fusion.50
  1372.9 42.4 %all-reduce.10.cloned.1.call-done = f32[393600]{0:T(1024)} async-done(((f32[393600]{0:T(1024)}), f32[393600]{0:T(1024)}) %all-reduce.10.cloned.1.call-update) | async-done | bytes 1574416 | tf_op jit(solution)/shard_map/psum | solution.py:38
  1415.2 0.7 slice.159
  1415.9 0.6 stack_reshape.16
  1416.6 1.0 slice.160
  1417.6 0.7 stack_reshape.17
  1418.3 1.5 fusion.105
  1419.8 0.9 stack_reshape.19
  1420.7 0.8 stack_reshape.15
  1421.5 0.9 stack_reshape.18
  1422.4 0.6 slice_bitcast_fusion.5
  1423.0 0.6 slice_bitcast_fusion.2
  (113 shorter events, 5.0 us)
Async XLA Ops:
  7.2 8.5 copy-start.17
  7.2 9.7 copy-start.19
  7.2 10.0 copy-start.20
  7.2 10.2 copy-start.21
  7.2 84.9 %copy-start.18 = (bf16[1,2,32]{2,1,0:T(2,128)(2,1)S(1)}, bf16[1,2,32]{2,1,0:T(2,128)(2,1)}, u32[]{:S(2)}) copy-start(bf16[1,2,32]{2,1,0:T(2,128)(2,1)} %param.19) | copy-start | bytes 388
  7.2 161.0 %all-gather.13.cloned.1.call-start = ((), (), s32[]{:S(2)}) async-start(), calls=%async_computation.9 | async-start | bytes 6488064 | tf_op jit(solution)/shard_map/all_gather | solution.py:254
  8.0 321.9 %all-gather.11.cloned.1.call-start = ((), (), s32[]{:S(2)}) async-start(), calls=%async_computation.5 | async-start | bytes 9732096 | tf_op jit(solution)/shard_map/all_gather | solution.py:17
  10.6 157.6 %copy-start = (bf16[1,128,1024]{2,1,0:T(8,128)(2,1)S(1)}, bf16[1,128,1024]{2,1,0:T(8,128)(2,1)}, u32[]{:S(2)}) copy-start(bf16[1,128,1024]{2,1,0:T(8,128)(2,1)} %param.15) | copy-start | bytes 786436
  10.6 495.1 %all-gather.9.cloned.1.call-start = ((), (), s32[]{:S(2)}) async-start(), calls=%async_computation.4 | async-start | bytes 11083776 | tf_op jit(solution)/shard_map/all_gather | solution.py:17
  14.9 723.0 %reduce-scatter.15.cloned.1.call-start = ((), (), s32[]{:S(2)}) async-start(), calls=%async_computation.11 | async-start | bytes 540672
  172.3 1.2 copy-start.15
  172.5 1.0 copy-start.14
  173.6 335.9 %copy-start.3 = (bf16[16,64,128]{2,1,0:T(8,128)(2,1)}, bf16[16,64,128]{2,1,0:T(8,128)(2,1)S(1)}, u32[]{:S(2)}) copy-start(bf16[16,64,128]{2,1,0:T(8,128)(2,1)S(1)} %convolution_convert_fusion.1) | copy-start | bytes 786436
  509.7 7.0 copy-start.16
  516.7 4.8 copy-start.1
  516.7 3.5 copy-start.2
  520.5 5.3 slice-start.1
  521.4 4.4 copy-start.5
  521.4 4.4 slice-start.2
  521.4 4.4 slice-start.3
  525.8 3.8 copy-start.12
  534.8 10.1 copy-start.8
  537.1 7.8 copy-start.10
  538.3 344.3 %reduce-scatter.13.cloned.1.call-start = ((), (), s32[]{:S(2)}) async-start(), calls=%async_computation.10 | async-start | bytes 12976128 | tf_op jit(solution)/shard_map/reduce_scatter | solution.py:303
  557.5 1.0 copy-start.6
  557.5 531.7 %reduce-scatter.11.cloned.1.call-start = ((), (), s32[]{:S(2)}) async-start(), calls=%async_computation.7 | async-start | bytes 17436672 | tf_op jit(solution)/shard_map/reduce_scatter | solution.py:28
  568.9 0.9 copy-start.4
  568.9 778.1 %reduce-scatter.9.cloned.1.call-start = ((), (), s32[]{:S(2)}) async-start(), calls=%async_computation.6 | async-start | bytes 22167552 | tf_op jit(solution)/shard_map/reduce_scatter | solution.py:28
  569.9 2.7 copy-start.13
  605.9 809.4 %all-reduce.10.cloned.1.call-start = ((), (), s32[]{:S(2)}) async-start(), calls=%async_computation.8 | async-start | bytes 3153920 | tf_op jit(solution)/shard_map/psum | solution.py:38
  1350.4 16.7 %copy-start.9 = (bf16[16,64,128]{2,1,0:T(8,128)(2,1)S(1)}, bf16[16,64,128]{2,1,0:T(8,128)(2,1)}, u32[]{:S(2)}) copy-start(bf16[16,64,128]{2,1,0:T(8,128)(2,1)} %copy-done.8) | copy-start | bytes 786436
  1350.4 16.7 %copy-start.11 = (bf16[1,128,16,64]{1,3,2,0:T(8,128)(2,1)S(1)}, bf16[1,128,16,64]{1,3,2,0:T(8,128)(2,1)}, u32[]{:S(2)}) copy-start(bf16[1,128,16,64]{1,3,2,0:T(8,128)(2,1)} %copy-done.10) | copy-start | bytes 786436
  1417.6 3.1 slice-start
  1419.8 2.6 copy-start.7
Sparse Core Ops, SparseCore 0:
  9.7 148.1 all-gather.12
  160.2 169.6 all-gather.10
  332.1 173.5 all-gather.8
  538.4 150.4 reduce-scatter.14
  691.3 191.2 reduce-scatter.12
  885.0 204.1 reduce-scatter.10
  1091.7 255.2 reduce-scatter.8
  1367.2 48.0 all-reduce.9
where the time goes:
time: 1440 us; the launch traced here: 1430 us
  waiting for transfers between devices  979 us (68%)
  blocking collectives  274 us (19%)
  local copies, waits for them, and re-layouts  87.5 us (6%)
  matrix products  58.9 us (4%)
  between operations  17 us (1%)
    reduce_scatter x2, waiting for transfers between devices, in_one_piece(): lax.psum_scatter(both, axis, scatter_dimension=dim, tiled=True)  461 us
    all_gather x2, waiting for transfers between devices, sent_together(): filled, at, done = (lax.all_gather(both, axis, axis=dim, tiled=True), 0, [])  331 us
    unnamed x2, blocking collectives  206 us
    reduce_scatter x1, waiting for transfers between devices, body(): lax.psum_scatter(terms[0], 'shard', scatter_dimension=0, tiled=True)  144 us
    all_gather x1, blocking collectives, body(): lax.all_gather(b_qv[layer_index], 'shard', axis=1, tiled=True)  68.2 us
    psum x1, waiting for transfers between devices, together(): so_far = lax.psum(line, axis)  42.4 us
  transfers between devices with their start and end apart: 8, of which 6 were waited for; matrix products, arithmetic and copies ran while one was open for 7% of the time, Pallas kernels for 0%

commit v1 on v0

--- a/solution.py
+++ b/solution.py
@@ -35,7 +35,11 @@
 
 def together(arrays, axis):
     line, at, done = (jnp.concatenate([a.reshape(-1) for a in arrays]), 0, [])
-    so_far = lax.psum(line, axis)
+
+    def use_bands(point, along_axis):
+        return jnp.sum(lax.all_gather(point, axis_name=along_axis), 0)
+
+    so_far = use_bands(line, axis)
     for a in arrays:
         done.append(so_far[at : at + a.size].reshape(a.shape))
         at += a.size

time: 1440 us -> 1470 us (1.021)
  other arithmetic: 14.2 us -> 44.6 us
    psum x1 -> x0, waiting for transfers between devices: 42.4 us -> none  [together(): so_far = lax.psum(line, axis)]
    all_gather x0 -> x1, waiting for transfers between devices: none -> 41.7 us  [use_bands(): return jnp.sum(lax.all_gather(point, axis_name=along_axis), 0)]
    reduce_sum x0 -> x1, other arithmetic: none -> 30.4 us  [use_bands(): return jnp.sum(lax.all_gather(point, axis_name=along_axis), 0)]
    unnamed x70 -> x69, local copies, waits for them, and re-layouts: 20.7 us -> 29.6 us
where the time goes in v1:
time: 1470 us; the launch traced here: 1460 us
  waiting for transfers between devices  978 us (67%)
  blocking collectives  274 us (19%)
  local copies, waits for them, and re-layouts  88.7 us (6%)
  matrix products  58.9 us (4%)
  other arithmetic  44.6 us (3%)
  between operations  16.9 us (1%)
    reduce_scatter x2, waiting for transfers between devices, in_one_piece(): lax.psum_scatter(both, axis, scatter_dimension=dim, tiled=True)  464 us
    all_gather x2, waiting for transfers between devices, sent_together(): filled, at, done = (lax.all_gather(both, axis, axis=dim, tiled=True), 0, [])  330 us
    unnamed x2, blocking collectives  206 us
    reduce_scatter x1, waiting for transfers between devices, body(): lax.psum_scatter(terms[0], 'shard', scatter_dimension=0, tiled=True)  142 us
    all_gather x1, blocking collectives, body(): lax.all_gather(b_qv[layer_index], 'shard', axis=1, tiled=True)  68.2 us
    all_gather x1, waiting for transfers between devices, use_bands(): return jnp.sum(lax.all_gather(point, axis_name=along_axis), 0)  41.7 us
    reduce_sum x1, other arithmetic, use_bands(): return jnp.sum(lax.all_gather(point, axis_name=along_axis), 0)  30.4 us
    unnamed x69, local copies, waits for them, and re-layouts  29.6 us
  transfers between devices with their start and end apart: 8, of which 6 were waited for; matrix products, arithmetic and copies ran while one was open for 7% of the time, Pallas kernels for 0%

profile of v1, /device:TPU:1, one launch (start us, length us, event | category | flops | bytes accessed | tf_op | source)
XLA Modules:
  0.0 1461.9 jit_solution(1826189338528841422)
XLA Ops:
  7.3 0.7 all-gather.16.cloned.1.call-update
  8.0 0.8 copy.91
  8.8 1.8 pad_maximum_fusion.4
  10.7 0.8 copy.88
  11.4 0.8 copy.89
  12.2 0.8 copy.90
  12.9 2.0 concatenate.21
  15.7 0.6 fusion.108
  17.6 74.4 %all-reduce.7 = (bf16[1024]{0:T(1024)(128)(2,1)S(1)}, bf16[1024]{0:T(1024)(128)(2,1)S(1)}, bf16[1024]{0:T(1024)(128)(2,1)S(1)}) all-reduce(bf16[1024]{0:T(1024)(128)(2,1)S(1)} %dynamic-update-slice, bf16[1024]{0:T(1024)(128)(2,1)S(1)} %dynamic-update-slice.2, ...), channel_id=4, replica_groups=mesh['rep'=4,'shard'=32] {'shard'}, use_global_device_ids=true, to_apply=%add | all-reduce | flops 3072 | bytes 12288
  92.2 68.2 %all-gather.1 = bf16[1,2,1024]{1,0,2:T(2,128)(2,1)S(1)} all-gather(bf16[1,2,32]{1,0,2:T(2,128)(2,1)S(1)} %copy.83), channel_id=3, replica_groups=mesh['rep'=4,'shard'=32] {'shard'}, dimensions={2}, use_global_device_ids=true | all-gather | bytes 4224 | tf_op jit(solution)/shard_map/all_gather | solution.py:259
  160.4 0.5 convert_element_type.136
  161.0 7.2 slice_reduce_fusion
  168.3 3.8 fusion.11
  172.7 0.4 fusion.109
  173.6 156.3 %all-gather.14.cloned.1.call-done = bf16[4096,1025]{1,0:T(8,128)(2,1)} async-done(((bf16[128,1025]{1,0:T(8,128)(2,1)}), bf16[4096,1025]{1,0:T(8,128)(2,1)}) %all-gather.14.cloned.1.call-update) | async-done | bytes 8396816 | tf_op jit(solution)/shard_map/all_gather | solution.py:17
  329.9 1.6 convert_reduce_fusion
  331.5 174.2 %all-gather.12.cloned.1.call-done = bf16[1024,5123]{1,0:T(8,128)(2,1)} async-done(((bf16[32,5123]{1,0:T(8,128)(2,1)}), bf16[1024,5123]{1,0:T(8,128)(2,1)}) %all-gather.12.cloned.1.call-update) | async-done | bytes 10491920 | tf_op jit(solution)/shard_map/all_gather | solution.py:17
  505.7 1.6 convert_reduce_fusion.3
  507.3 2.1 fusion.110
  509.7 6.9 fusion.13
  516.7 3.2 fusion.111
  520.5 1.0 fusion.102
  521.4 4.3 fusion.114
  525.8 3.7 multiply_reduce_fusion.1
  529.8 0.8 fusion.53
  530.8 0.6 fusion.107
  531.3 1.3 fusion.115
  532.7 2.1 convolution_convert_fusion
  534.8 2.3 fusion.106
  537.3 1.0 copy.109
  538.5 6.4 convolution_bitcast_fusion
  544.9 12.6 copy.107
  557.6 1.0 copy-done.6
  558.5 4.0 fusion.91
  562.5 6.4 pad_maximum_fusion
  569.9 2.7 fusion.88
  572.6 8.3 fusion.73
  580.8 25.0 %concatenate.24 = f32[1024,5123]{1,0:T(8,128)} concatenate(f32[1024,1024]{1,0:T(8,128)} %fusion.88, f32[1024,1]{1,0:T(8,128)S(1)} %copy.98, f32[1024,1]{1,0:T(8,128)S(1)} %copy.99, f32[1024,1]{1,0:T(8,128)S(1)} %copy.100, f32[1024,4096]{1,0:T(8,128)} %fusion.73), dimensions={1} | concatenate | bytes 41967616 | tf_op jit(solution)/shard_map/concatenate | solution.py:27
  606.6 131.1 %all-reduce.6 = (f32[1024]{0:T(1024)S(1)}, f32[1024]{0:T(1024)S(1)}, f32[1024]{0:T(1024)S(1)}) all-reduce(f32[1024]{0:T(1024)S(1)} %get-tuple-element.35, f32[1024]{0:T(1024)S(1)} %get-tuple-element.19, f32[1024]{0:T(1024)S(1)} %convert_reduce_fusion.1), channel_id=12, replica_groups=mesh['rep'=4,'shard'=32] {'shard'}, use_global_device_ids=true, to_apply=%region_22.23.clone | all-reduce | flops 3072 | bytes 24576
  738.0 0.8 copy.110
  738.8 0.6 reshape.292
  739.4 141.9 %reduce-scatter.13.cloned.1.call-done = f32[32,3072]{1,0:T(8,128)} async-done(((f32[1024,3072]{1,0:T(8,128)}), f32[32,3072]{1,0:T(8,128)}) %reduce-scatter.13.cloned.1.call-update) | async-done | bytes 393232 | tf_op jit(solution)/shard_map/reduce_scatter | solution.py:307
  881.3 1.1 copy.111
  882.3 207.8 %reduce-scatter.11.cloned.1.call-done = f32[128,1025]{0,1:T(8,128)} async-done(((f32[4096,1025]{0,1:T(8,128)}), f32[128,1025]{0,1:T(8,128)}) %reduce-scatter.11.cloned.1.call-update) | async-done | bytes 524816 | tf_op jit(solution)/shard_map/reduce_scatter | solution.py:28
  1090.1 1.1 slice.157
  1091.5 1.2 slice_bitcast_fusion.9
  1092.7 255.8 %reduce-scatter.9.cloned.1.call-done = f32[32,5123]{1,0:T(8,128)} async-done(((f32[1024,5123]{1,0:T(8,128)}), f32[32,5123]{1,0:T(8,128)}) %reduce-scatter.9.cloned.1.call-update) | async-done | bytes 655760 | tf_op jit(solution)/shard_map/reduce_scatter | solution.py:28
  1348.5 1.2 slice_bitcast_fusion
  1349.7 0.9 copy.113
  1350.6 0.9 slice_bitcast_fusion.1
  1351.6 1.1 slice_reduce_fusion.2
  1352.7 10.6 concatenate.26
  1363.3 8.1 reshape.331
  1371.4 5.8 fusion.50
  1377.2 41.7 %all-gather.18.cloned.1.call-done = f32[4,1,393600]{2,1,0:T(1,128)} async-done(((f32[1,1,393600]{2,1,0:T(1,128)}), f32[4,1,393600]{2,1,0:T(1,128)}) %all-gather.18.cloned.1.call-update) | async-done | bytes 6297616 | tf_op jit(solution)/shard_map/all_gather | solution.py:40
  1418.9 30.4 %reduce_sum.199 = f32[393600]{0:T(1024)S(1)} reduce(f32[4,1,393600]{2,1,0:T(1,128)} %all-gather.18.cloned.1.call-done, f32[]{:T(128)} %constant.22.clone.1), dimensions={0,1}, to_apply=%region_27.28 | reduce | flops 1180800 | bytes 7872004 | tf_op jit(solution)/shard_map/reduce_sum | solution.py:40
  1449.3 0.6 slice_bitcast_fusion.5
  1449.9 0.6 slice_bitcast_fusion.2
  1450.6 0.3 fusion.105
  1451.0 0.6 stack_reshape.16
  1451.6 0.7 stack_reshape.17
  1452.3 0.9 stack_reshape.19
  1453.2 0.8 stack_reshape.15
  1454.0 0.9 stack_reshape.18
  (112 shorter events, 5.5 us)
Async XLA Ops:
  7.2 8.5 copy-start.16
  7.2 9.7 copy-start.18
  7.2 10.0 copy-start.19
  7.2 10.2 copy-start.20
  7.2 84.9 %copy-start.17 = (bf16[1,2,32]{2,1,0:T(2,128)(2,1)S(1)}, bf16[1,2,32]{2,1,0:T(2,128)(2,1)}, u32[]{:S(2)}) copy-start(bf16[1,2,32]{2,1,0:T(2,128)(2,1)} %param.19) | copy-start | bytes 388
  7.2 161.0 %all-gather.16.cloned.1.call-start = ((), (), s32[]{:S(2)}) async-start(), calls=%async_computation.8 | async-start | bytes 6488064 | tf_op jit(solution)/shard_map/all_gather | solution.py:258
  8.0 321.9 %all-gather.14.cloned.1.call-start = ((), (), s32[]{:S(2)}) async-start(), calls=%async_computation.5 | async-start | bytes 9732096 | tf_op jit(solution)/shard_map/all_gather | solution.py:17
  10.6 157.6 %copy-start = (bf16[1,128,1024]{2,1,0:T(8,128)(2,1)S(1)}, bf16[1,128,1024]{2,1,0:T(8,128)(2,1)}, u32[]{:S(2)}) copy-start(bf16[1,128,1024]{2,1,0:T(8,128)(2,1)} %param.15) | copy-start | bytes 786436
  10.6 495.1 %all-gather.12.cloned.1.call-start = ((), (), s32[]{:S(2)}) async-start(), calls=%async_computation.4 | async-start | bytes 11083776 | tf_op jit(solution)/shard_map/all_gather | solution.py:17
  14.9 723.0 %reduce-scatter.15.cloned.1.call-start = ((), (), s32[]{:S(2)}) async-start(), calls=%async_computation.11 | async-start | bytes 540672
  172.4 1.2 copy-start.14
  172.6 1.1 copy-start.13
  173.6 335.8 %copy-start.3 = (bf16[16,64,128]{2,1,0:T(8,128)(2,1)}, bf16[16,64,128]{2,1,0:T(8,128)(2,1)S(1)}, u32[]{:S(2)}) copy-start(bf16[16,64,128]{2,1,0:T(8,128)(2,1)S(1)} %convolution_convert_fusion.1) | copy-start | bytes 786436
  509.7 7.0 copy-start.15
  516.7 4.8 copy-start.1
  516.7 3.5 copy-start.2
  520.5 5.3 slice-start
  521.4 4.4 copy-start.5
  521.4 4.4 slice-start.1
  521.4 4.4 slice-start.2
  525.8 3.7 copy-start.11
  534.8 10.1 copy-start.7
  537.1 7.8 copy-start.9
  538.3 343.0 %reduce-scatter.13.cloned.1.call-start = ((), (), s32[]{:S(2)}) async-start(), calls=%async_computation.10 | async-start | bytes 12976128 | tf_op jit(solution)/shard_map/reduce_scatter | solution.py:307
  557.5 1.0 copy-start.6
  557.5 532.6 %reduce-scatter.11.cloned.1.call-start = ((), (), s32[]{:S(2)}) async-start(), calls=%async_computation.7 | async-start | bytes 17436672 | tf_op jit(solution)/shard_map/reduce_scatter | solution.py:28
  568.9 0.9 copy-start.4
  569.0 779.5 %reduce-scatter.9.cloned.1.call-start = ((), (), s32[]{:S(2)}) async-start(), calls=%async_computation.6 | async-start | bytes 22167552 | tf_op jit(solution)/shard_map/reduce_scatter | solution.py:28
  569.9 2.7 copy-start.12
  605.9 813.0 %all-gather.18.cloned.1.call-start = ((), (), s32[]{:S(2)}) async-start(), calls=%async_computation.9 | async-start | bytes 7872000 | tf_op jit(solution)/shard_map/all_gather | solution.py:40
  1363.3 8.1 copy-start.8
  1363.3 8.1 copy-start.10
Sparse Core Ops, SparseCore 0:
  9.7 148.1 all-gather.15
  160.2 169.6 all-gather.13
  332.1 173.5 all-gather.11
  538.4 150.4 reduce-scatter.14
  691.3 189.8 reduce-scatter.12
  883.7 206.4 reduce-scatter.10
  1092.7 255.7 reduce-scatter.8
  1371.5 47.3 all-gather.17
